TPU v7x, 512 devices: a whole 4x8x8 slice. The times are simulated.
512 devices in a mesh: req: 64 (over x, y, core), head: 8 (over z).
Axes of the slice: x: 4, y: 8, z: 8, core: 2. Of those that a mesh axis runs over, the one named last changes fastest.
Arguments:
- hidden: bfloat16 [512, 4096], P(None, 'req'), may hold values from -16 to 16
- query_key_value_weight: bfloat16 [4096, 8, 768], P('req', 'head'), may hold values from -0.1875 to 0.1875
- output_weight: bfloat16 [4096, 4096], P('head', 'req'), may hold values from -0.375 to 0.375
- kv_pool: bfloat16 [4096, 8, 128, 256], P('req', 'head'), may hold values from -68 to 68
- lengths: int32 [512], P('req'), may hold values from 513 to 2048, as said below
- page_table: int32 [512, 16], P('req'), may hold values from 0 to 127, as said below
- send_slots: int32 [4096], P('req'), may hold values from 0 to 63, as said below
Outputs:
- attn_out: bfloat16 [512, 4096], P('head', 'req')
Inputs may be any that keep to these rules, and one draw needn't show every extreme that they name: `page_table`: A request's live positions name distinct slots of its group's store, and every other entry is 0. Slots below 64 are the group's own pool rows; slot 64 + s is the page that group s sends to it. Every group uses exactly 32 of the 64 pages sent to it, never for a long request. `send_slots`: every group sends one page to every group; rows whose page the receiver does not use name an arbitrary slot. In 16 of the groups one request is long (more than (15) * 128 tokens); all others hold at most 768 tokens. The new token sits at position lengths[r].
All inputs are finite; a program needn't handle non-finite values.
Results may differ from a plain program's by a relative error of at most 0.018.
Values may be sent and summed in bfloat16 or wider, within the bound.
A program may use at most 64 MiB of HBM per device.

v0:
```python
import jax
import jax.numpy as jnp
from jax import lax
from jax.sharding import PartitionSpec as P

ROPE_BASE = 500000.0
NEG_FILL = -1e30


def rotate(vectors, angles):
    half_width = vectors.shape[-1] // 2
    first_half = vectors[..., :half_width]
    second_half = vectors[..., half_width:]
    cosine = jnp.cos(angles)
    sine_part = jnp.sin(angles)
    return jnp.concatenate(
        [
            first_half * cosine - second_half * sine_part,
            second_half * cosine + first_half * sine_part,
        ],
        axis=-1,
    )


def rope_angles(lengths, width):
    exponent = jnp.arange(width // 2, dtype=jnp.float32) * (2.0 / width)
    inverse = 1.0 / ROPE_BASE**exponent
    return lengths.astype(jnp.float32)[:, None] * inverse[None, :]


def split_projection(projected_rows, lengths):
    angles = rope_angles(lengths, projected_rows.shape[-1])
    queries = rotate(projected_rows[:, :, :-2], angles[:, None, None, :]).astype(jnp.bfloat16)
    new_keys = rotate(projected_rows[:, :, -2], angles[:, None, :]).astype(jnp.bfloat16)
    new_values = projected_rows[:, :, -1].astype(jnp.bfloat16)
    return (queries, new_keys, new_values)


def page_stats(queries, pages, valid_tokens, score_scale):
    head_dim = pages.shape[-1] // 2
    scores = (
        jnp.einsum(
            "nhqd,nhtd->nhqt", queries, pages[..., :head_dim], preferred_element_type=jnp.float32
        )
        * score_scale
    )
    token_mask = jnp.arange(pages.shape[2])[None, None, None, :] < valid_tokens[:, None, None, None]
    masked = jnp.where(token_mask, scores, NEG_FILL)
    top_score = jnp.max(masked, axis=-1)
    weights = jnp.where(token_mask, jnp.exp(scores - top_score[..., None]), 0.0)
    weight_sum = jnp.sum(weights, axis=-1)
    weighted_values = jnp.einsum(
        "nhqt,nhtd->nhqd",
        weights.astype(jnp.bfloat16),
        pages[..., head_dim:],
        preferred_element_type=jnp.float32,
    )
    return (top_score, weight_sum, weighted_values)


def shards(hidden, query_key_value_weight, output_weight, kv_pool, lengths, page_table, send_slots):
    groups = lax.axis_size("req")
    local_count = lengths.shape[0]
    head_count = query_key_value_weight.shape[1]
    pool_slots = kv_pool.shape[0]
    page_len = kv_pool.shape[2]
    head_dim = kv_pool.shape[3] // 2
    per_head = query_key_value_weight.shape[2] // head_dim
    flat_weight = query_key_value_weight.reshape(
        query_key_value_weight.shape[0], head_count * per_head * head_dim
    )
    projected_rows = lax.psum_scatter(
        jnp.dot(hidden, flat_weight, preferred_element_type=jnp.float32),
        "req",
        scatter_dimension=0,
        tiled=True,
    )
    projected_rows = projected_rows.reshape(local_count, head_count, per_head, head_dim)
    queries, new_keys, new_values = split_projection(projected_rows, lengths)
    score_scale = head_dim ** (-0.5)
    self_scores = (
        jnp.sum(queries.astype(jnp.float32) * new_keys.astype(jnp.float32)[:, :, None, :], axis=-1)
        * score_scale
    )
    total_slots = pool_slots + groups
    places = jnp.arange(page_table.shape[1], dtype=jnp.int32)
    is_live = places[None, :] * page_len < lengths[:, None]
    tokens_in = jnp.clip(lengths[:, None] - places[None, :] * page_len, 0, page_len)
    table_hits = (
        page_table[:, :, None] == jnp.arange(total_slots, dtype=jnp.int32)[None, None, :]
    ) & is_live[:, :, None]
    owner_map = jnp.any(table_hits, axis=1).T
    valid_tokens = jnp.sum(jnp.where(table_hits, tokens_in[:, :, None], 0), axis=(0, 1))
    owner_index = jnp.sum(
        jnp.where(owner_map, jnp.arange(local_count, dtype=jnp.int32)[None, :], 0), axis=1
    )
    slot_queries = jnp.einsum(
        "nr,rhqd->nhqd", owner_map.astype(jnp.bfloat16), queries, preferred_element_type=jnp.float32
    ).astype(jnp.bfloat16)
    outgoing = kv_pool[send_slots]
    arrived = lax.all_to_all(outgoing, "req", split_axis=0, concat_axis=0, tiled=True)
    page_store = jnp.concatenate([kv_pool, arrived], axis=0)
    page_max, page_sum, page_acc = page_stats(slot_queries, page_store, valid_tokens, score_scale)
    owned_max = jnp.max(jnp.where(owner_map[:, :, None, None], page_max[:, None], NEG_FILL), axis=0)
    top_score = jnp.maximum(owned_max, self_scores)
    factors = jnp.exp(page_max - top_score[owner_index])
    owner_float = owner_map.astype(jnp.float32)
    self_weight = jnp.exp(self_scores - top_score)
    total_weight_sum = (
        jnp.einsum("nr,nhq->rhq", owner_float, factors * page_sum, precision=lax.Precision.HIGHEST)
        + self_weight
    )
    weighted_values = jnp.einsum(
        "nr,nhqd->rhqd", owner_float, factors[..., None] * page_acc, precision=lax.Precision.HIGHEST
    )
    weighted_values = (
        weighted_values + self_weight[..., None] * new_values.astype(jnp.float32)[:, :, None, :]
    )
    output_per_head = (
        (weighted_values / total_weight_sum[..., None])
        .astype(jnp.bfloat16)
        .reshape(local_count, head_count * (per_head - 2) * head_dim)
    )
    partial_out = jnp.dot(
        lax.all_gather(output_per_head, "req", axis=0, tiled=True),
        output_weight,
        preferred_element_type=jnp.float32,
    )
    return lax.psum_scatter(
        partial_out.astype(jnp.bfloat16), "head", scatter_dimension=0, tiled=True
    )


def solution(mesh):
    return jax.shard_map(
        shards,
        mesh=mesh,
        in_specs=(
            P(None, "req"),
            P("req", "head", None),
            P("head", "req"),
            P("req", "head", None, None),
            P("req"),
            P("req", None),
            P("req"),
        ),
        out_specs=P("head", "req"),
        check_vma=False,
    )
```

profile of v0, /device:TPU:2, one launch (start us, length us, event | category | flops | bytes accessed | tf_op | source)
XLA Modules:
  0.0 291.1 jit_solution(14235447509010207527)
XLA Ops:
  6.5 0.0 copy-start
  6.5 0.7 compare_select_fusion.1
  7.2 5.0 %gather_fusion = bf16[64,128,256]{2,1,0:T(8,128)(2,1)} fusion(bf16[64,128,256]{2,1,0:T(8,128)(2,1)} %bitcast.50, s32[1024]{0:T(1024)S(1)} %pad_clamp_fusion.1), kind=kCustom, calls=%fused_computation | custom fusion | bytes 8388864 | tf_op jit(solution)/shard_map/gather | solution.py:100
  12.2 0.0 copy-start.2
  12.2 0.0 copy-start.4
  12.2 0.0 copy-start.3
  12.2 11.1 %all-to-all-start = ((bf16[64,1,128,256]{3,2,1,0:T(8,128)(2,1)}), bf16[64,1,128,256]{3,2,1,0:T(8,128)(2,1)}, u32[]{:S(2)}, u32[]{:S(2)}) async-start(bf16[64,1,128,256]{3,2,1,0:T(8,128)(2,1)} %bitcast.53), calls=%async_computation.1 | async-start | bytes 8388608 | tf_op jit(solution)/shard_map/all_to_all | solution.py:101
  23.4 0.0 reduce-scatter.3.cloned.1.call-start
  23.4 0.0 copy-done
  23.4 0.0 copy-done.2
  23.4 1.6 fusion.25
  25.0 0.0 reduce-scatter.3.cloned.1.call-update
  25.1 0.0 reduce-scatter.5.cloned.1.call-start
  25.1 0.0 copy-done.4
  25.2 0.1 broadcast_compare_fusion
  25.2 0.0 copy-done.3
  25.2 0.1 fusion.29
  25.4 0.1 subtract_clamp_fusion
  25.5 0.1 select_reduce_fusion.1
  25.6 0.1 multiply_cosine_fusion.1
  25.7 0.1 iota_compare_fusion
  25.8 155.3 %reduce-scatter.3.cloned.1.call-done = f32[8,768]{1,0:T(8,128)} async-done(((f32[512,768]{1,0:T(8,128)}), f32[8,768]{1,0:T(8,128)}) %reduce-scatter.3.cloned.1.call-update) | async-done | bytes 24592 | tf_op jit(solution)/shard_map/reduce_scatter | solution.py:72
  181.1 0.7 slice_bitcast_fusion
  181.8 0.1 fusion.46
  181.9 0.1 maximum_convert_fusion
  182.0 0.9 subtract_convert_fusion
  182.9 0.2 multiply_reduce_fusion
  183.0 0.7 fusion.44
  183.7 0.3 convolution_convert_fusion.1
  184.0 0.0 all-to-all-done
  184.0 4.6 %select_reduce_fusion = (f32[128,4]{1,0:T(8,128)S(1)}, f32[128,4,128]{2,1,0:T(4,128)S(1)}) fusion(pred[128,128]{1,0:T(8,128)(4,1)S(1)} %iota_compare_fusion, bf16[64,1,128,256]{3,2,0,1:T(8,128)(2,1)} %bitcast.51, bf16[64,1,128,256]{3,2,0,1:T(8,128)(2,1)} %bitcast.8, bf16[128,4,128]{2,0,1:T(8,128)(2,1)S(1)} %convolution_convert_fusion.1), kind=kOutput, calls=%fused_computation.22 | convolution fusion | flops 19070464 | bytes 8800256 | tf_op jit(solution)/shard_map/nhqd,nhtd->nhqt/dot_general | solution.py:42
  188.6 0.1 copy.20
  188.6 0.1 select_reduce_fusion.2
  188.8 0.1 copy.21
  188.8 0.7 gather_fusion.1
  189.5 0.4 fusion.18
  189.9 0.0 copy-start.1
  189.9 3.5 %fusion.11 = f32[128,4,128]{2,1,0:T(4,128)S(1)} fusion(bf16[64,1,128,256]{3,2,0,1:T(8,128)(2,1)} %bitcast.8, bf16[64,1,128,256]{3,2,0,1:T(8,128)(2,1)} %bitcast.52, f32[128,4,128]{2,1,0:T(4,128)S(1)} %get-tuple-element.14, f32[128,4]{1,0:T(8,128)S(1)} %get-tuple-element.13, f32[128,4]{1,0:T(8,128)S(1)} %subtract_exponential_fusion, ...), kind=kOutput, calls=%fused_computation.12 | convolution fusion | flops 25427968 | bytes 8933376 | tf_op jit(solution)/shard_map/nhqt,nhtd->nhqd/dot_general | solution.py:52
  193.4 0.2 convolution_add_fusion.1
  193.6 0.2 fusion.16
  193.9 48.6 %all_gather.3 = bf16[512,512]{1,0:T(8,128)(2,1)S(1)} all-gather(bf16[8,512]{1,0:T(8,128)(2,1)S(1)} %fusion.16), channel_id=1, replica_groups=mesh['req'=64,'head'=8] {'req'}, dimensions={0}, use_global_device_ids=true | all-gather | bytes 532480 | tf_op jit(solution)/shard_map/all_gather | solution.py:125
  242.5 0.0 copy-done.1
  242.5 0.9 convolution_convert_fusion
  243.4 0.0 reduce-scatter.5.cloned.1.call-update
  243.4 40.8 %reduce-scatter.5.cloned.1.call-done = bf16[64,64]{1,0:T(8,128)(2,1)} async-done(((bf16[512,64]{1,0:T(8,128)(2,1)}), bf16[64,64]{1,0:T(8,128)(2,1)}) %reduce-scatter.5.cloned.1.call-update) | async-done | bytes 8208 | tf_op jit(solution)/shard_map/reduce_scatter | solution.py:129
  (9 shorter events, 0.1 us)
Async XLA Ops:
  6.5 16.9 %copy-start = (bf16[64,1,768]{2,0,1:T(8,128)(2,1)S(1)}, bf16[64,1,768]{2,0,1:T(8,128)(2,1)}, u32[]{:S(2)}) copy-start(bf16[64,1,768]{2,0,1:T(8,128)(2,1)} %param.8) | copy-start | bytes 294916
  12.2 11.2 %copy-start.2 = (bf16[512,64]{0,1:T(8,128)(2,1)S(1)}, bf16[512,64]{0,1:T(8,128)(2,1)}, u32[]{:S(2)}) copy-start(bf16[512,64]{0,1:T(8,128)(2,1)} %param.7) | copy-start | bytes 196612
  12.2 12.9 %copy-start.4 = (s32[8]{0:T(128)S(1)}, s32[8]{0:T(128)}, u32[]{:S(2)}) copy-start(s32[8]{0:T(128)} %param.11) | copy-start | bytes 100
  12.2 13.0 %copy-start.3 = (s32[8,16]{1,0:T(8,128)S(1)}, s32[8,16]{1,0:T(8,128)}, u32[]{:S(2)}) copy-start(s32[8,16]{1,0:T(8,128)} %param.12) | copy-start | bytes 1540
  12.2 171.8 %all-to-all-start = ((bf16[64,1,128,256]{3,2,1,0:T(8,128)(2,1)}), bf16[64,1,128,256]{3,2,1,0:T(8,128)(2,1)}, u32[]{:S(2)}, u32[]{:S(2)}) async-start(bf16[64,1,128,256]{3,2,1,0:T(8,128)(2,1)} %bitcast.53), calls=%async_computation.1 | async-start | bytes 8388608 | tf_op jit(solution)/shard_map/all_to_all | solution.py:101
  23.4 157.7 %reduce-scatter.3.cloned.1.call-start = ((), (), s32[]{:S(2)}) async-start(), calls=%async_computation.3 | async-start | bytes 1597440 | tf_op jit(solution)/shard_map/reduce_scatter | solution.py:72
  25.1 259.2 %reduce-scatter.5.cloned.1.call-start = ((), (), s32[]{:S(2)}) async-start(), calls=%async_computation.4 | async-start | bytes 147456 | tf_op jit(solution)/shard_map/reduce_scatter | solution.py:129
  189.9 52.6 %copy-start.1 = (bf16[512,64]{0,1:T(8,128)(2,1)S(1)}, bf16[512,64]{0,1:T(8,128)(2,1)}, u32[]{:S(2)}) copy-start(bf16[512,64]{0,1:T(8,128)(2,1)} %param.9) | copy-start | bytes 196612
Sparse Core Ops, SparseCore 0:
  28.8 152.2 reduce-scatter.2
  243.6 40.6 reduce-scatter.4
where the time goes:
time: 292 us; the launch traced here: 291 us
  waiting for transfers between devices  196 us (67%)
  blocking collectives  48.6 us (17%)
  between operations  13.5 us (5%)
  matrix products  11.3 us (4%)
  starting transfers between devices  11.2 us (4%)
  local copies, waits for them, and re-layouts  6.47 us (2%)
  other arithmetic  3.76 us (1%)
    reduce_scatter x1, waiting for transfers between devices, shards(): lax.psum_scatter(jnp.dot(hidden, flat_weight, preferred_element_type=jnp....  155 us
    all_gather x1, blocking collectives, shards(): lax.all_gather(output_per_head, 'req', axis=0, tiled=True)  48.6 us
    reduce_scatter x1, waiting for transfers between devices, shards(): lax.psum_scatter(partial_out.astype(jnp.bfloat16), 'head', scatter_dimens...  40.8 us
    all_to_all x1, starting transfers between devices, shards(): lax.all_to_all(outgoing, 'req', split_axis=0, concat_axis=0, tiled=True)  11.1 us
  transfers between devices with their start and end apart: 3, of which 2 were waited for; matrix products, arithmetic and copies ran while one was open for 2% of the time, Pallas kernels for 0%

commit v1 on v0

--- a/solution.py
+++ b/solution.py
@@ -121,10 +121,11 @@
         .astype(jnp.bfloat16)
         .reshape(local_count, head_count * (per_head - 2) * head_dim)
     )
+    name_heads_all = lambda t0, d0: jnp.concatenate(
+        lax.all_to_all(jnp.stack([t0 for _ in range(lax.axis_size("req"))]), "req", 0, 0), d0
+    )
     partial_out = jnp.dot(
-        lax.all_gather(output_per_head, "req", axis=0, tiled=True),
-        output_weight,
-        preferred_element_type=jnp.float32,
+        name_heads_all(output_per_head, 0), output_weight, preferred_element_type=jnp.float32
     )
     return lax.psum_scatter(
         partial_out.astype(jnp.bfloat16), "head", scatter_dimension=0, tiled=True

time: 292 us -> 266 us (0.911)
  blocking collectives: 48.6 us -> 25.1 us
    all_gather x1 -> x0, blocking collectives: 48.6 us -> none  [shards(): lax.all_gather(output_per_head, 'req', axis=0, tiled=True)]
    all_to_all x0 -> x1, blocking collectives: none -> 25.1 us  [shards(): lax.all_to_all(jnp.stack([t0 for _ in range(lax.axis_size('req'))]), 'req...]
where the time goes in v1:
time: 266 us; the launch traced here: 265 us
  waiting for transfers between devices  194 us (73%)
  blocking collectives  25.1 us (9%)
  between operations  13.5 us (5%)
  matrix products  11.3 us (4%)
  starting transfers between devices  11.2 us (4%)
  local copies, waits for them, and re-layouts  6.51 us (2%)
  other arithmetic  3.76 us (1%)
    reduce_scatter x1, waiting for transfers between devices, shards(): lax.psum_scatter(jnp.dot(hidden, flat_weight, preferred_element_type=jnp....  155 us
    reduce_scatter x1, waiting for transfers between devices, shards(): lax.psum_scatter(partial_out.astype(jnp.bfloat16), 'head', scatter_dimens...  38.5 us
    all_to_all x1, blocking collectives, shards(): lax.all_to_all(jnp.stack([t0 for _ in range(lax.axis_size('req'))]), 'req...  25.1 us
    all_to_all x1, starting transfers between devices, shards(): lax.all_to_all(outgoing, 'req', split_axis=0, concat_axis=0, tiled=True)  11.1 us
  transfers between devices with their start and end apart: 3, of which 2 were waited for; matrix products, arithmetic and copies ran while one was open for 2% of the time, Pallas kernels for 0%

profile of v1, /device:TPU:2, one launch (start us, length us, event | category | flops | bytes accessed | tf_op | source)
XLA Modules:
  0.0 265.3 jit_solution(14369854928838752136)
XLA Ops:
  6.5 0.0 copy-start
  6.5 0.7 compare_select_fusion.1
  7.2 5.0 %gather_fusion = bf16[64,128,256]{2,1,0:T(8,128)(2,1)} fusion(bf16[64,128,256]{2,1,0:T(8,128)(2,1)} %bitcast.52, s32[1024]{0:T(1024)S(1)} %pad_clamp_fusion.1), kind=kCustom, calls=%fused_computation | custom fusion | bytes 8388864 | tf_op jit(solution)/shard_map/gather | solution.py:100
  12.2 0.0 copy-start.2
  12.2 0.0 copy-start.4
  12.2 0.0 copy-start.3
  12.2 11.1 %all-to-all-start = ((bf16[64,1,128,256]{3,2,1,0:T(8,128)(2,1)}), bf16[64,1,128,256]{3,2,1,0:T(8,128)(2,1)}, u32[]{:S(2)}, u32[]{:S(2)}) async-start(bf16[64,1,128,256]{3,2,1,0:T(8,128)(2,1)} %bitcast.55), calls=%async_computation.1 | async-start | bytes 8388608 | tf_op jit(solution)/shard_map/all_to_all | solution.py:101
  23.4 0.0 reduce-scatter.3.cloned.1.call-start
  23.4 0.0 copy-done
  23.4 0.0 copy-done.2
  23.4 1.6 fusion.26
  25.0 0.0 reduce-scatter.3.cloned.1.call-update
  25.1 0.0 reduce-scatter.5.cloned.1.call-start
  25.1 0.0 copy-done.4
  25.2 0.1 broadcast_compare_fusion
  25.2 0.0 copy-done.3
  25.2 0.1 fusion.30
  25.4 0.1 subtract_clamp_fusion
  25.5 0.1 select_reduce_fusion.1
  25.6 0.1 multiply_cosine_fusion.1
  25.7 0.1 iota_compare_fusion
  25.8 155.3 %reduce-scatter.3.cloned.1.call-done = f32[8,768]{1,0:T(8,128)} async-done(((f32[512,768]{1,0:T(8,128)}), f32[8,768]{1,0:T(8,128)}) %reduce-scatter.3.cloned.1.call-update) | async-done | bytes 24592 | tf_op jit(solution)/shard_map/reduce_scatter | solution.py:72
  181.1 0.7 slice_bitcast_fusion
  181.8 0.1 fusion.47
  181.9 0.1 maximum_convert_fusion
  182.0 0.9 subtract_convert_fusion
  182.9 0.2 multiply_reduce_fusion
  183.0 0.7 fusion.45
  183.7 0.3 convolution_convert_fusion.1
  184.0 0.0 all-to-all-done
  184.0 4.6 %select_reduce_fusion = (f32[128,4]{1,0:T(8,128)S(1)}, f32[128,4,128]{2,1,0:T(4,128)S(1)}) fusion(pred[128,128]{1,0:T(8,128)(4,1)S(1)} %iota_compare_fusion, bf16[64,1,128,256]{3,2,0,1:T(8,128)(2,1)} %bitcast.53, bf16[64,1,128,256]{3,2,0,1:T(8,128)(2,1)} %bitcast.8, bf16[128,4,128]{2,0,1:T(8,128)(2,1)S(1)} %convolution_convert_fusion.1), kind=kOutput, calls=%fused_computation.23 | convolution fusion | flops 19070464 | bytes 8800256 | tf_op jit(solution)/shard_map/nhqd,nhtd->nhqt/dot_general | solution.py:42
  188.6 0.1 copy.20
  188.6 0.1 select_reduce_fusion.2
  188.8 0.1 copy.21
  188.8 0.7 gather_fusion.1
  189.5 0.4 fusion.19
  189.9 0.0 copy-start.1
  189.9 3.5 %fusion.11 = f32[128,4,128]{2,1,0:T(4,128)S(1)} fusion(bf16[64,1,128,256]{3,2,0,1:T(8,128)(2,1)} %bitcast.8, bf16[64,1,128,256]{3,2,0,1:T(8,128)(2,1)} %bitcast.54, f32[128,4,128]{2,1,0:T(4,128)S(1)} %get-tuple-element.14, f32[128,4]{1,0:T(8,128)S(1)} %get-tuple-element.13, f32[128,4]{1,0:T(8,128)S(1)} %subtract_exponential_fusion, ...), kind=kOutput, calls=%fused_computation.12 | convolution fusion | flops 25427968 | bytes 8933376 | tf_op jit(solution)/shard_map/nhqt,nhtd->nhqd/dot_general | solution.py:52
  193.4 0.2 convolution_add_fusion.1
  193.6 0.2 fusion.16
  193.9 25.1 %all_to_all.10 = bf16[64,8,512]{2,1,0:T(8,128)(2,1)S(1)} all-to-all(bf16[64,8,512]{2,1,0:T(8,128)(2,1)S(1)} %stack.3), channel_id=1, replica_groups=mesh['req'=64,'head'=8] {'req'}, dimensions={0} | all-to-all | bytes 1048576 | tf_op jit(solution)/shard_map/all_to_all | solution.py:125
  219.0 0.0 copy-done.1
  219.0 0.9 convolution_convert_fusion
  219.9 0.0 reduce-scatter.5.cloned.1.call-update
  219.9 38.5 %reduce-scatter.5.cloned.1.call-done = bf16[64,64]{1,0:T(8,128)(2,1)} async-done(((bf16[512,64]{1,0:T(8,128)(2,1)}), bf16[64,64]{1,0:T(8,128)(2,1)}) %reduce-scatter.5.cloned.1.call-update) | async-done | bytes 8208 | tf_op jit(solution)/shard_map/reduce_scatter | solution.py:130
  (10 shorter events, 0.1 us)
Async XLA Ops:
  6.5 16.9 %copy-start = (bf16[64,1,768]{2,0,1:T(8,128)(2,1)S(1)}, bf16[64,1,768]{2,0,1:T(8,128)(2,1)}, u32[]{:S(2)}) copy-start(bf16[64,1,768]{2,0,1:T(8,128)(2,1)} %param.8) | copy-start | bytes 294916
  12.2 11.2 %copy-start.2 = (bf16[512,64]{0,1:T(8,128)(2,1)S(1)}, bf16[512,64]{0,1:T(8,128)(2,1)}, u32[]{:S(2)}) copy-start(bf16[512,64]{0,1:T(8,128)(2,1)} %param.7) | copy-start | bytes 196612
  12.2 12.9 %copy-start.4 = (s32[8]{0:T(128)S(1)}, s32[8]{0:T(128)}, u32[]{:S(2)}) copy-start(s32[8]{0:T(128)} %param.11) | copy-start | bytes 100
  12.2 13.0 %copy-start.3 = (s32[8,16]{1,0:T(8,128)S(1)}, s32[8,16]{1,0:T(8,128)}, u32[]{:S(2)}) copy-start(s32[8,16]{1,0:T(8,128)} %param.12) | copy-start | bytes 1540
  12.2 171.8 %all-to-all-start = ((bf16[64,1,128,256]{3,2,1,0:T(8,128)(2,1)}), bf16[64,1,128,256]{3,2,1,0:T(8,128)(2,1)}, u32[]{:S(2)}, u32[]{:S(2)}) async-start(bf16[64,1,128,256]{3,2,1,0:T(8,128)(2,1)} %bitcast.55), calls=%async_computation.1 | async-start | bytes 8388608 | tf_op jit(solution)/shard_map/all_to_all | solution.py:101
  23.4 157.7 %reduce-scatter.3.cloned.1.call-start = ((), (), s32[]{:S(2)}) async-start(), calls=%async_computation.4 | async-start | bytes 1597440 | tf_op jit(solution)/shard_map/reduce_scatter | solution.py:72
  25.1 233.4 %reduce-scatter.5.cloned.1.call-start = ((), (), s32[]{:S(2)}) async-start(), calls=%async_computation.5 | async-start | bytes 147456 | tf_op jit(solution)/shard_map/reduce_scatter | solution.py:130
  189.9 29.1 %copy-start.1 = (bf16[512,64]{0,1:T(8,128)(2,1)S(1)}, bf16[512,64]{0,1:T(8,128)(2,1)}, u32[]{:S(2)}) copy-start(bf16[512,64]{0,1:T(8,128)(2,1)} %param.9) | copy-start | bytes 196612
Sparse Core Ops, SparseCore 0:
  28.8 152.2 reduce-scatter.2
  220.1 38.3 reduce-scatter.4
